TPU v7x, 512 devices: a whole 4x8x8 slice. The times are simulated.
512 devices in a mesh: gx: 16 (over z, core), gy: 32 (over y, x).
Axes of the slice: x: 4, y: 8, z: 8, core: 2. Of those that a mesh axis runs over, the one named last changes fastest.
Arguments:
- positions: float32 [3, 16, 32, 4096], P(None, 'gx', 'gy'), may hold values from 0 to 2
- velocities: float32 [3, 16, 32, 4096], P(None, 'gx', 'gy'), may hold values from -6 to 6
- mass: float32 [16, 32, 4096], P('gx', 'gy'), may hold values from 0.05 to 0.3
- stiffness: float32 [16, 32, 4096], P('gx', 'gy'), may hold values from 0.5 to 8
- counts: int32 [16, 32, 32], P('gx', 'gy'), may hold values from 32 to 128
- pairs: int32 [65536, 2], P(('gx', 'gy')), may hold values from 0 to 16383, as said below
- pair_count: int32 [512], P(('gx', 'gy')), may hold values from 32 to 128, as said below
Outputs:
- new_positions: float32 [3, 16, 32, 4096], P(None, 'gx', 'gy')
- new_velocities: float32 [3, 16, 32, 4096], P(None, 'gx', 'gy')
- density: float32 [16, 32, 4096], P('gx', 'gy')
Inputs may be any that keep to these rules, and one draw needn't show every extreme that they name: `pairs`: box d's list is rows d * 128 to (d + 1) * 128 - 1, box d being (d // 32, d % 32). Its first 32 rows pair each of the box's own tiles with itself, in order. In every other row the first tile lies in a box with the same gy index and a gx index at most one away, the second tile in a box with the same gx index and a gy index at most one away. Rows may repeat. `pair_count`: some box has 128 live rows in every draw.
All inputs are finite; a program needn't handle non-finite values.
Results may differ from a plain program's by a relative error of at most 0.0001.
Values sent between devices are 32-bit elements; how exact they have to be, the bound alone decides.
A program may use at most 64 MiB of HBM per device.

v0:
```python
import math

import jax
import jax.numpy as jnp
from jax import lax
from jax.sharding import PartitionSpec as P

kernel_norm = 21.0 / (16.0 * math.pi)
viscosity = 0.1
time_step = 0.02
rest_density = 1.0


def passed_along(block, axis, distance):
    devices = range(lax.axis_size(axis))
    route = [(i - distance, i) for i in devices if i - distance in devices]
    return lax.ppermute(block, axis, route)


def with_halo(value, sides, width):
    edges = {}
    for axis, dim in sides:
        devices, length = (lax.axis_size(axis), value.shape[dim])
        up = [(i, (i + 1) % devices) for i in range(devices - 1)]
        last = lax.slice_in_dim(value, length - width, length, axis=dim)
        initial = lax.slice_in_dim(value, 0, width, axis=dim)
        edges[dim] = (
            lax.ppermute(last, axis, up),
            lax.ppermute(initial, axis, [(b, a) for a, b in up]),
        )
    done = []
    for _, dim in sides:
        low, high = edges[dim]
        around = [(width, width) if d in done else (0, 0) for d in range(value.ndim)]
        value = jnp.concatenate([jnp.pad(low, around), value, jnp.pad(high, around)], axis=dim)
        done.append(dim)
    return value


def kernel_terms(points_a, points_b):
    offset = points_a[:, :, :, None] - points_b[:, :, None, :]
    distance = jnp.sqrt(jnp.sum(offset * offset, axis=0))
    falloff = jnp.maximum(1.0 - 0.5 * distance, 0.0)
    weight = kernel_norm * falloff**4 * (2.0 * distance + 1.0)
    slope = -5.0 * kernel_norm * falloff**3
    return (offset, weight, slope)


def density_terms(points_a, points_b, mass_a, mass_b, live_rows, cross_rows):
    offset, weight, slope = kernel_terms(points_a, points_b)
    to_first = jnp.sum(weight * mass_b[:, None, :], axis=2) * live_rows[:, None]
    to_second = jnp.sum(weight * mass_a[:, :, None], axis=1) * cross_rows[:, None]
    return (to_first, to_second)


def force_terms(
    points_a,
    points_b,
    speed_a,
    speed_b,
    mass_a,
    mass_b,
    press_a,
    press_b,
    scale_a,
    scale_b,
    live_rows,
    cross_rows,
):
    offset, weight, slope = kernel_terms(points_a, points_b)
    push = -(press_a[:, :, None] + press_b[:, None, :])
    drag = 2.0 * viscosity / (scale_a[:, :, None] * scale_b[:, None, :])
    relative = speed_a[:, :, :, None] - speed_b[:, :, None, :]
    force = slope[None] * (push[None] * offset + drag[None] * relative)
    to_first = jnp.sum(force * mass_b[None, :, None, :], axis=3) * live_rows[None, :, None]
    to_second = -jnp.sum(force * mass_a[None, :, :, None], axis=2) * cross_rows[None, :, None]
    return (to_first, to_second)


def run_pairs(update, initial, row_total):

    def turn(turn_index, totals):
        return update(totals, turn_index * 8)

    return lax.fori_loop(0, (row_total + 7) // 8, turn, initial)


def send_back(tower_part, plate_part, width_gy):
    own_part = tower_part[:, 1] + plate_part[:, 1]
    total_part = own_part
    for piece, offset in (
        (tower_part[:, 0], -width_gy),
        (tower_part[:, 2], width_gy),
        (plate_part[:, 0], -1),
        (plate_part[:, 2], 1),
    ):
        total_part = total_part + passed_along(piece, ("gx", "gy"), offset)
    return total_part


def body(positions, velocities, mass, stiffness, counts, pairs, pair_count):
    tiles_here = counts.shape[2]
    slot_count = positions.shape[3]
    tile_size = slot_count // tiles_here
    width_gy = lax.axis_size("gy")
    row_here = lax.axis_index("gx")
    column_here = lax.axis_index("gy")
    slot_index = jnp.arange(tile_size, dtype=jnp.int32)
    validity = (
        (slot_index[None, :] < counts.reshape(tiles_here, 1))
        .astype(jnp.float32)
        .reshape(slot_count)
    )
    points = positions.reshape(3, slot_count)
    speeds = velocities.reshape(3, slot_count)
    weighted = mass.reshape(slot_count) * validity
    packed = jnp.concatenate([points, speeds, weighted[None]], axis=0).reshape(7, 1, 1, slot_count)
    beside_all = with_halo(packed, (("gx", 1), ("gy", 2)), 1)
    tower = beside_all[:, :, 1, :].reshape(7, 3 * tiles_here, tile_size)
    plate = beside_all[:, 1, :, :].reshape(7, 3 * tiles_here, tile_size)
    first_tiles = pairs[:, 0]
    second_tiles = pairs[:, 1]
    first_local = (
        first_tiles // tiles_here // width_gy - row_here + 1
    ) * tiles_here + first_tiles % tiles_here
    second_local = (
        second_tiles // tiles_here % width_gy - column_here + 1
    ) * tiles_here + second_tiles % tiles_here
    row_limit = pairs.shape[0]
    live_count = pair_count[0]
    live_flag = (jnp.arange(row_limit, dtype=jnp.int32) < live_count).astype(jnp.float32)
    cross_flag = jnp.where(first_tiles != second_tiles, live_flag, 0.0 * live_flag)

    def block_rows(begin_row):
        return (
            lax.dynamic_slice_in_dim(first_local, begin_row, 8),
            lax.dynamic_slice_in_dim(second_local, begin_row, 8),
            lax.dynamic_slice_in_dim(live_flag, begin_row, 8),
            lax.dynamic_slice_in_dim(cross_flag, begin_row, 8),
        )

    def density_update(totals, begin_row):
        first_ids, second_ids, live_rows, cross_rows = block_rows(begin_row)
        side_a = jnp.take(tower, first_ids, axis=1)
        side_b = jnp.take(plate, second_ids, axis=1)
        to_first, to_second = density_terms(
            side_a[0:3], side_b[0:3], side_a[6], side_b[6], live_rows, cross_rows
        )
        return (totals[0].at[first_ids].add(to_first), totals[1].at[second_ids].add(to_second))

    blank_sums = jnp.zeros((3 * tiles_here, tile_size), jnp.float32)
    tower_sums, plate_sums = run_pairs(density_update, (blank_sums, blank_sums), live_count)
    density = send_back(
        tower_sums.reshape(1, 3, slot_count), plate_sums.reshape(1, 3, slot_count), width_gy
    )[0]
    scale = density + 1.0 - validity
    press = stiffness.reshape(slot_count) * (density - rest_density) / (scale * scale)
    fetched = with_halo(
        jnp.stack([press, scale], axis=0).reshape(2, 1, 1, slot_count), (("gx", 1), ("gy", 2)), 1
    )
    tower_extra = fetched[:, :, 1, :].reshape(2, 3 * tiles_here, tile_size)
    plate_extra = fetched[:, 1, :, :].reshape(2, 3 * tiles_here, tile_size)

    def force_update(totals, begin_row):
        first_ids, second_ids, live_rows, cross_rows = block_rows(begin_row)
        side_a = jnp.take(tower, first_ids, axis=1)
        side_b = jnp.take(plate, second_ids, axis=1)
        extra_a = jnp.take(tower_extra, first_ids, axis=1)
        extra_b = jnp.take(plate_extra, second_ids, axis=1)
        to_first, to_second = force_terms(
            side_a[0:3],
            side_b[0:3],
            side_a[3:6],
            side_b[3:6],
            side_a[6],
            side_b[6],
            extra_a[0],
            extra_b[0],
            extra_a[1],
            extra_b[1],
            live_rows,
            cross_rows,
        )
        return (
            totals[0].at[:, first_ids].add(to_first),
            totals[1].at[:, second_ids].add(to_second),
        )

    blank_accel = jnp.zeros((3, 3 * tiles_here, tile_size), jnp.float32)
    tower_accel, plate_accel = run_pairs(force_update, (blank_accel, blank_accel), live_count)
    accel = send_back(
        tower_accel.reshape(3, 3, slot_count), plate_accel.reshape(3, 3, slot_count), width_gy
    )
    new_speeds = speeds + time_step * validity[None] * accel
    new_points = points + time_step * new_speeds
    return (
        new_points.reshape(positions.shape),
        new_speeds.reshape(velocities.shape),
        density.reshape(mass.shape),
    )


def solution(mesh):
    placed = (
        P(None, "gx", "gy", None),
        P(None, "gx", "gy", None),
        P("gx", "gy", None),
        P("gx", "gy", None),
        P("gx", "gy", None),
        P(("gx", "gy"), None),
        P(("gx", "gy")),
    )
    return jax.shard_map(
        body,
        mesh=mesh,
        in_specs=placed,
        out_specs=(P(None, "gx", "gy", None), P(None, "gx", "gy", None), P("gx", "gy", None)),
        check_vma=False,
    )
```

profile of v0, /device:TPU:33, one launch (start us, length us, event | category | flops | bytes accessed | tf_op | source)
XLA Modules:
  0.0 261.3 jit_solution(9537424634118319422)
XLA Ops:
  0.6 0.7 fusion.26
  1.4 0.7 bitcast_select_fusion
  2.1 0.9 copy_bitcast_fusion
  3.1 2.6 collective-permute-start.1
  5.7 3.9 %collective-permute-start = (f32[7,1,1,4096]{3,0,2,1:T(8,128)S(1)}, f32[7,1,1,4096]{3,0,2,1:T(8,128)S(1)}, u32[]{:S(2)}, u32[]{:S(2)}) collective-permute-start(f32[7,1,1,4096]{3,0,2,1:T(8,128)S(1)} %maximum_bitcast_fusion), channel_id=1, source_target_pairs={{0,32},{32,64},{64,96},{96,128},{128,160},{160,192},{192,224},{224... | collective-permute-start | bytes 344072 | tf_op jit(solution)/shard_map/ppermute | solution.py:28
  9.6 4.3 %collective-permute-start.3 = (f32[7,1,1,4096]{3,0,2,1:T(8,128)S(1)}, f32[7,1,1,4096]{3,0,2,1:T(8,128)S(1)}, u32[]{:S(2)}, u32[]{:S(2)}) collective-permute-start(f32[7,1,1,4096]{3,0,2,1:T(8,128)S(1)} %maximum_bitcast_fusion), channel_id=1, source_target_pairs={{1,0},{2,1},{3,2},{4,3},{5,4},{6,5},{7,6},{8,7},{9,8},{10,9},{11,1... | collective-permute-start | bytes 344072 | tf_op jit(solution)/shard_map/ppermute | solution.py:29
  13.9 1.9 collective-permute-start.2
  16.6 7.0 %collective-permute-done.2 = f32[7,1,1,4096]{3,0,2,1:T(8,128)S(1)} collective-permute-done((f32[7,1,1,4096]{3,0,2,1:T(8,128)S(1)}, f32[7,1,1,4096]{3,0,2,1:T(8,128)S(1)}, u32[]{:S(2)}, u32[]{:S(2)}) %collective-permute-start.2) | collective-permute-done | bytes 114720 | tf_op jit(solution)/shard_map/ppermute | solution.py:28
  23.6 51.8 %while.24 = (s32[]{:T(128)}, f32[96,128]{1,0:T(8,128)S(1)}, f32[96,128]{1,0:T(8,128)S(1)}, s32[]{:T(128)}, s32[128]{0:T(128)S(1)}, /*index=5*/f32[7,96,128]{2,0,...) while((s32[]{:T(128)}, f32[96,128]{1,0:T(8,128)S(1)}, ...), condition=%wide.region_6.8_spmd, body=%wide.region_0.7_spmd.sunk | while | flops 2771046 | bytes 1549927 | solution.py:85
  75.5 1.9 collective-permute-start.7
  77.5 6.7 %collective-permute-start.6 = (f32[1,4096]{1,0:T(1,128)S(1)}, f32[1,4096]{1,0:T(1,128)S(1)}, u32[]{:S(2)}, u32[]{:S(2)}) collective-permute-start(f32[1,4096]{1,0:T(1,128)S(1)} %get-tuple-element.249), channel_id=1, source_target_pairs={{1,0},{2,1},{3,2},{4,3},{5,4},{6,5},{7,6},{8,7},{9,8},{10,9},{11,1... | collective-permute-start | bytes 49160 | tf_op jit(solution)/shard_map/ppermute | solution.py:17
  84.2 16.4 %collective-permute-start.5 = (f32[1,4096]{1,0:T(1,128)S(1)}, f32[1,4096]{1,0:T(1,128)S(1)}, u32[]{:S(2)}, u32[]{:S(2)}) collective-permute-start(f32[1,4096]{1,0:T(1,128)S(1)} %get-tuple-element.248), channel_id=1, source_target_pairs={{0,32},{1,33},{2,34},{3,35},{4,36},{5,37},{6,38},{7,39},{8,40},{9,... | collective-permute-start | bytes 49160 | tf_op jit(solution)/shard_map/ppermute | solution.py:17
  100.6 1.9 collective-permute-start.4
  102.6 3.1 %collective-permute-done.4 = f32[1,4096]{1,0:T(1,128)S(1)} collective-permute-done((f32[1,4096]{1,0:T(1,128)S(1)}, f32[1,4096]{1,0:T(1,128)S(1)}, u32[]{:S(2)}, u32[]{:S(2)}) %collective-permute-start.4) | collective-permute-done | bytes 16416 | tf_op jit(solution)/shard_map/ppermute | solution.py:17
  105.8 1.9 collective-permute-start.9
  107.8 3.6 %collective-permute-start.8 = (f32[2,1,1,4096]{3,0,2,1:T(2,128)S(1)}, f32[2,1,1,4096]{3,0,2,1:T(2,128)S(1)}, u32[]{:S(2)}, u32[]{:S(2)}) collective-permute-start(f32[2,1,1,4096]{3,0,2,1:T(2,128)S(1)} %maximum_bitcast_fusion.1), channel_id=1, source_target_pairs={{0,32},{32,64},{64,96},{96,128},{128,160},{160,192},{192,224},{224... | collective-permute-start | bytes 98312 | tf_op jit(solution)/shard_map/ppermute | solution.py:28
  111.4 1.9 collective-permute-start.11
  113.3 3.4 %collective-permute-start.10 = (f32[2,1,1,4096]{3,0,2,1:T(2,128)S(1)}, f32[2,1,1,4096]{3,0,2,1:T(2,128)S(1)}, u32[]{:S(2)}, u32[]{:S(2)}) collective-permute-start(f32[2,1,1,4096]{3,0,2,1:T(2,128)S(1)} %maximum_bitcast_fusion.1), channel_id=1, source_target_pairs={{0,1},{1,2},{2,3},{3,4},{4,5},{5,6},{6,7},{7,8},{8,9},{9,10},{10,1... | collective-permute-start | bytes 98312 | tf_op jit(solution)/shard_map/ppermute | solution.py:28
  116.8 4.5 %collective-permute-done.10 = f32[2,1,1,4096]{3,0,2,1:T(2,128)S(1)} collective-permute-done((f32[2,1,1,4096]{3,0,2,1:T(2,128)S(1)}, f32[2,1,1,4096]{3,0,2,1:T(2,128)S(1)}, u32[]{:S(2)}, u32[]{:S(2)}) %collective-permute-start.10) | collective-permute-done | bytes 32800 | tf_op jit(solution)/shard_map/ppermute | solution.py:28
  121.4 97.9 %while.25 = (s32[]{:T(128)}, f32[3,96,128]{2,0,1:T(4,128)S(1)}, f32[3,96,128]{2,0,1:T(4,128)S(1)}, s32[]{:T(128)}, s32[128]{0:T(128)S(1)}, /*index=5*/f32[7,96,1...) while((s32[]{:T(128)}, f32[3,96,128]{2,0,1:T(4,128)S(1)}, ...), condition=%wide.region_13.16_spmd, body=%wide.region_7.15_spmd.sunk | while | flops 6321254 | bytes 5038919 | solution.py:85
  125.4 1.6 multiply_reduce_fusion.10
  127.2 0.8 scatter_fusion
  128.2 0.8 scatter_fusion.1
  132.9 1.6 multiply_reduce_fusion.10
  134.8 0.8 scatter_fusion
  135.7 0.8 scatter_fusion.1
  140.5 1.6 multiply_reduce_fusion.10
  142.3 0.8 scatter_fusion
  143.2 0.8 scatter_fusion.1
  148.0 1.6 multiply_reduce_fusion.10
  149.8 0.8 scatter_fusion
  150.8 0.8 scatter_fusion.1
  155.5 1.6 multiply_reduce_fusion.10
  157.3 0.8 scatter_fusion
  158.3 0.8 scatter_fusion.1
  163.0 1.6 multiply_reduce_fusion.10
  164.9 0.8 scatter_fusion
  165.8 0.8 scatter_fusion.1
  170.6 1.6 multiply_reduce_fusion.10
  172.4 0.8 scatter_fusion
  173.3 0.8 scatter_fusion.1
  178.1 1.6 multiply_reduce_fusion.10
  179.9 0.8 scatter_fusion
  180.9 0.8 scatter_fusion.1
  185.6 1.6 multiply_reduce_fusion.10
  187.4 0.8 scatter_fusion
  188.4 0.8 scatter_fusion.1
  193.2 1.6 multiply_reduce_fusion.10
  195.0 0.8 scatter_fusion
  195.9 0.8 scatter_fusion.1
  200.7 1.6 multiply_reduce_fusion.10
  202.5 0.8 scatter_fusion
  203.5 0.8 scatter_fusion.1
  208.2 1.6 multiply_reduce_fusion.10
  210.0 0.8 scatter_fusion
  211.0 0.8 scatter_fusion.1
  215.7 1.6 multiply_reduce_fusion.10
  217.6 0.8 scatter_fusion
  218.5 0.8 scatter_fusion.1
  219.4 1.9 collective-permute-start.15
  221.3 6.7 %collective-permute-start.14 = (f32[3,4096]{1,0:T(4,128)S(1)}, f32[3,4096]{1,0:T(4,128)S(1)}, u32[]{:S(2)}, u32[]{:S(2)}) collective-permute-start(f32[3,4096]{1,0:T(4,128)S(1)} %get-tuple-element.245), channel_id=1, source_target_pairs={{1,0},{2,1},{3,2},{4,3},{5,4},{6,5},{7,6},{8,7},{9,8},{10,9},{11,1... | collective-permute-start | bytes 147464 | tf_op jit(solution)/shard_map/ppermute | solution.py:17
  228.0 26.2 %collective-permute-start.13 = (f32[3,4096]{1,0:T(4,128)S(1)}, f32[3,4096]{1,0:T(4,128)S(1)}, u32[]{:S(2)}, u32[]{:S(2)}) collective-permute-start(f32[3,4096]{1,0:T(4,128)S(1)} %get-tuple-element.244), channel_id=1, source_target_pairs={{0,32},{1,33},{2,34},{3,35},{4,36},{5,37},{6,38},{7,39},{8,40},{9,... | collective-permute-start | bytes 147464 | tf_op jit(solution)/shard_map/ppermute | solution.py:17
  254.2 1.9 collective-permute-start.12
  256.3 3.6 %collective-permute-done.12 = f32[3,4096]{1,0:T(4,128)S(1)} collective-permute-done((f32[3,4096]{1,0:T(4,128)S(1)}, f32[3,4096]{1,0:T(4,128)S(1)}, u32[]{:S(2)}, u32[]{:S(2)}) %collective-permute-start.12) | collective-permute-done | bytes 49184 | tf_op jit(solution)/shard_map/ppermute | solution.py:17
  (699 shorter events, 106.3 us)
Async XLA Ops:
  0.6 15.8 %copy-start.4 = (s32[128,2]{0,1:T(2,128)S(1)}, s32[128,2]{0,1:T(2,128)}, u32[]{:S(2)}) copy-start(s32[128,2]{0,1:T(2,128)} %param.20) | copy-start | bytes 3076
  3.1 13.4 %collective-permute-start.1 = (f32[7,1,1,4096]{3,0,2,1:T(8,128)S(1)}, f32[7,1,1,4096]{3,0,2,1:T(8,128)S(1)}, u32[]{:S(2)}, u32[]{:S(2)}) collective-permute-start(f32[7,1,1,4096]{3,0,2,1:T(8,128)S(1)} %maximum_bitcast_fusion), channel_id=1, source_target_pairs={{32,0},{64,32},{96,64},{128,96},{160,128},{192,160},{224,192},{256... | collective-permute-start | bytes 344072 | tf_op jit(solution)/shard_map/ppermute | solution.py:29
  5.7 10.9 %collective-permute-start = (f32[7,1,1,4096]{3,0,2,1:T(8,128)S(1)}, f32[7,1,1,4096]{3,0,2,1:T(8,128)S(1)}, u32[]{:S(2)}, u32[]{:S(2)}) collective-permute-start(f32[7,1,1,4096]{3,0,2,1:T(8,128)S(1)} %maximum_bitcast_fusion), channel_id=1, source_target_pairs={{0,32},{32,64},{64,96},{96,128},{128,160},{160,192},{192,224},{224... | collective-permute-start | bytes 344072 | tf_op jit(solution)/shard_map/ppermute | solution.py:28
  9.6 7.0 %collective-permute-start.3 = (f32[7,1,1,4096]{3,0,2,1:T(8,128)S(1)}, f32[7,1,1,4096]{3,0,2,1:T(8,128)S(1)}, u32[]{:S(2)}, u32[]{:S(2)}) collective-permute-start(f32[7,1,1,4096]{3,0,2,1:T(8,128)S(1)} %maximum_bitcast_fusion), channel_id=1, source_target_pairs={{1,0},{2,1},{3,2},{4,3},{5,4},{6,5},{7,6},{8,7},{9,8},{10,9},{11,1... | collective-permute-start | bytes 344072 | tf_op jit(solution)/shard_map/ppermute | solution.py:29
  13.9 9.7 %collective-permute-start.2 = (f32[7,1,1,4096]{3,0,2,1:T(8,128)S(1)}, f32[7,1,1,4096]{3,0,2,1:T(8,128)S(1)}, u32[]{:S(2)}, u32[]{:S(2)}) collective-permute-start(f32[7,1,1,4096]{3,0,2,1:T(8,128)S(1)} %maximum_bitcast_fusion), channel_id=1, source_target_pairs={{0,1},{1,2},{2,3},{3,4},{4,5},{5,6},{6,7},{7,8},{8,9},{9,10},{10,1... | collective-permute-start | bytes 344072 | tf_op jit(solution)/shard_map/ppermute | solution.py:28
  23.6 82.0 %copy-start.3 = (f32[1,1,4096]{2,1,0:T(1,128)S(1)}, f32[1,1,4096]{2,1,0:T(1,128)}, u32[]{:S(2)}) copy-start(f32[1,1,4096]{2,1,0:T(1,128)} %param.18) | copy-start | bytes 49156
  75.5 27.0 %collective-permute-start.7 = (f32[1,4096]{1,0:T(1,128)S(1)}, f32[1,4096]{1,0:T(1,128)S(1)}, u32[]{:S(2)}, u32[]{:S(2)}) collective-permute-start(f32[1,4096]{1,0:T(1,128)S(1)} %get-tuple-element.250), channel_id=1, source_target_pairs={{0,1},{1,2},{2,3},{3,4},{4,5},{5,6},{6,7},{7,8},{8,9},{9,10},{10,1... | collective-permute-start | bytes 49160 | tf_op jit(solution)/shard_map/ppermute | solution.py:17
  77.5 25.1 %collective-permute-start.6 = (f32[1,4096]{1,0:T(1,128)S(1)}, f32[1,4096]{1,0:T(1,128)S(1)}, u32[]{:S(2)}, u32[]{:S(2)}) collective-permute-start(f32[1,4096]{1,0:T(1,128)S(1)} %get-tuple-element.249), channel_id=1, source_target_pairs={{1,0},{2,1},{3,2},{4,3},{5,4},{6,5},{7,6},{8,7},{9,8},{10,9},{11,1... | collective-permute-start | bytes 49160 | tf_op jit(solution)/shard_map/ppermute | solution.py:17
  84.2 18.3 %collective-permute-start.5 = (f32[1,4096]{1,0:T(1,128)S(1)}, f32[1,4096]{1,0:T(1,128)S(1)}, u32[]{:S(2)}, u32[]{:S(2)}) collective-permute-start(f32[1,4096]{1,0:T(1,128)S(1)} %get-tuple-element.248), channel_id=1, source_target_pairs={{0,32},{1,33},{2,34},{3,35},{4,36},{5,37},{6,38},{7,39},{8,40},{9,... | collective-permute-start | bytes 49160 | tf_op jit(solution)/shard_map/ppermute | solution.py:17
  100.6 5.1 %collective-permute-start.4 = (f32[1,4096]{1,0:T(1,128)S(1)}, f32[1,4096]{1,0:T(1,128)S(1)}, u32[]{:S(2)}, u32[]{:S(2)}) collective-permute-start(f32[1,4096]{1,0:T(1,128)S(1)} %get-tuple-element.247), channel_id=1, source_target_pairs={{32,0},{33,1},{34,2},{35,3},{36,4},{37,5},{38,6},{39,7},{40,8},{41... | collective-permute-start | bytes 49160 | tf_op jit(solution)/shard_map/ppermute | solution.py:17
  105.7 15.7 %copy-start.2 = (f32[1,4096]{1,0:T(1,128)}, f32[1,4096]{1,0:T(1,128)S(1)}, u32[]{:S(2)}) copy-start(f32[1,4096]{1,0:T(1,128)S(1)} %get-tuple-element.230) | copy-start | bytes 49156
  105.8 10.9 %collective-permute-start.9 = (f32[2,1,1,4096]{3,0,2,1:T(2,128)S(1)}, f32[2,1,1,4096]{3,0,2,1:T(2,128)S(1)}, u32[]{:S(2)}, u32[]{:S(2)}) collective-permute-start(f32[2,1,1,4096]{3,0,2,1:T(2,128)S(1)} %maximum_bitcast_fusion.1), channel_id=1, source_target_pairs={{32,0},{64,32},{96,64},{128,96},{160,128},{192,160},{224,192},{256... | collective-permute-start | bytes 98312 | tf_op jit(solution)/shard_map/ppermute | solution.py:29
  107.8 9.0 %collective-permute-start.8 = (f32[2,1,1,4096]{3,0,2,1:T(2,128)S(1)}, f32[2,1,1,4096]{3,0,2,1:T(2,128)S(1)}, u32[]{:S(2)}, u32[]{:S(2)}) collective-permute-start(f32[2,1,1,4096]{3,0,2,1:T(2,128)S(1)} %maximum_bitcast_fusion.1), channel_id=1, source_target_pairs={{0,32},{32,64},{64,96},{96,128},{128,160},{160,192},{192,224},{224... | collective-permute-start | bytes 98312 | tf_op jit(solution)/shard_map/ppermute | solution.py:28
  111.4 5.4 %collective-permute-start.11 = (f32[2,1,1,4096]{3,0,2,1:T(2,128)S(1)}, f32[2,1,1,4096]{3,0,2,1:T(2,128)S(1)}, u32[]{:S(2)}, u32[]{:S(2)}) collective-permute-start(f32[2,1,1,4096]{3,0,2,1:T(2,128)S(1)} %maximum_bitcast_fusion.1), channel_id=1, source_target_pairs={{1,0},{2,1},{3,2},{4,3},{5,4},{6,5},{7,6},{8,7},{9,8},{10,9},{11,1... | collective-permute-start | bytes 98312 | tf_op jit(solution)/shard_map/ppermute | solution.py:29
  113.3 8.0 %collective-permute-start.10 = (f32[2,1,1,4096]{3,0,2,1:T(2,128)S(1)}, f32[2,1,1,4096]{3,0,2,1:T(2,128)S(1)}, u32[]{:S(2)}, u32[]{:S(2)}) collective-permute-start(f32[2,1,1,4096]{3,0,2,1:T(2,128)S(1)} %maximum_bitcast_fusion.1), channel_id=1, source_target_pairs={{0,1},{1,2},{2,3},{3,4},{4,5},{5,6},{6,7},{7,8},{8,9},{9,10},{10,1... | collective-permute-start | bytes 98312 | tf_op jit(solution)/shard_map/ppermute | solution.py:28
  219.3 36.9 %copy-start.5 = (s32[1,1,32]{2,1,0:T(1,128)S(1)}, s32[1,1,32]{2,1,0:T(1,128)}, u32[]{:S(2)}) copy-start(s32[1,1,32]{2,1,0:T(1,128)} %param.19) | copy-start | bytes 388
  219.3 40.5 %copy-start = (f32[3,1,1,4096]{3,2,1,0:T(1,128)S(1)}, f32[3,1,1,4096]{3,2,1,0:T(1,128)}, u32[]{:S(2)}) copy-start(f32[3,1,1,4096]{3,2,1,0:T(1,128)} %param.15) | copy-start | bytes 147460
  219.3 40.5 %copy-start.1 = (f32[3,1,1,4096]{3,2,1,0:T(1,128)S(1)}, f32[3,1,1,4096]{3,2,1,0:T(1,128)}, u32[]{:S(2)}) copy-start(f32[3,1,1,4096]{3,2,1,0:T(1,128)} %param.16) | copy-start | bytes 147460
  219.4 36.9 %collective-permute-start.15 = (f32[3,4096]{1,0:T(4,128)S(1)}, f32[3,4096]{1,0:T(4,128)S(1)}, u32[]{:S(2)}, u32[]{:S(2)}) collective-permute-start(f32[3,4096]{1,0:T(4,128)S(1)} %get-tuple-element.246), channel_id=1, source_target_pairs={{0,1},{1,2},{2,3},{3,4},{4,5},{5,6},{6,7},{7,8},{8,9},{9,10},{10,1... | collective-permute-start | bytes 147464 | tf_op jit(solution)/shard_map/ppermute | solution.py:17
  221.3 35.0 %collective-permute-start.14 = (f32[3,4096]{1,0:T(4,128)S(1)}, f32[3,4096]{1,0:T(4,128)S(1)}, u32[]{:S(2)}, u32[]{:S(2)}) collective-permute-start(f32[3,4096]{1,0:T(4,128)S(1)} %get-tuple-element.245), channel_id=1, source_target_pairs={{1,0},{2,1},{3,2},{4,3},{5,4},{6,5},{7,6},{8,7},{9,8},{10,9},{11,1... | collective-permute-start | bytes 147464 | tf_op jit(solution)/shard_map/ppermute | solution.py:17
  228.0 28.2 %collective-permute-start.13 = (f32[3,4096]{1,0:T(4,128)S(1)}, f32[3,4096]{1,0:T(4,128)S(1)}, u32[]{:S(2)}, u32[]{:S(2)}) collective-permute-start(f32[3,4096]{1,0:T(4,128)S(1)} %get-tuple-element.244), channel_id=1, source_target_pairs={{0,32},{1,33},{2,34},{3,35},{4,36},{5,37},{6,38},{7,39},{8,40},{9,... | collective-permute-start | bytes 147464 | tf_op jit(solution)/shard_map/ppermute | solution.py:17
  254.2 5.6 %collective-permute-start.12 = (f32[3,4096]{1,0:T(4,128)S(1)}, f32[3,4096]{1,0:T(4,128)S(1)}, u32[]{:S(2)}, u32[]{:S(2)}) collective-permute-start(f32[3,4096]{1,0:T(4,128)S(1)} %get-tuple-element.243), channel_id=1, source_target_pairs={{32,0},{33,1},{34,2},{35,3},{36,4},{37,5},{38,6},{39,7},{40,8},{41... | collective-permute-start | bytes 147464 | tf_op jit(solution)/shard_map/ppermute | solution.py:17
where the time goes:
time: 260 us; the launch traced here: 261 us
  other arithmetic  98.5 us (38%)
  starting transfers between devices  87.1 us (34%)
  local copies, waits for them, and re-layouts  51.8 us (20%)
  waiting for transfers between devices  18.2 us (7%)
  loops' own time  4 us (2%)
    ppermute x8, starting transfers between devices, passed_along(): return lax.ppermute(block, axis, route)  63.6 us
    reduce_sum x13, other arithmetic, force_terms(): jnp.sum(force * mass_a[None, :, :, None], axis=2)  21.4 us
    ppermute x4, starting transfers between devices, with_halo(): lax.ppermute(last, axis, up)  12.8 us
    reduce_sum x26, other arithmetic, kernel_terms(): distance = jnp.sqrt(jnp.sum(offset * offset, axis=0))  12.3 us
    ppermute x4, waiting for transfers between devices, with_halo(): lax.ppermute(last, axis, up)  11.5 us
    ppermute x4, starting transfers between devices, with_halo(): lax.ppermute(initial, axis, [(b, a) for a, b in up])  10.7 us
    scatter-add x13, other arithmetic, force_update(): totals[1].at[:, second_ids].add(to_second)  10.1 us
    scatter-add x13, other arithmetic, force_update(): totals[0].at[:, first_ids].add(to_first)  10.1 us
  transfers between devices with their start and end apart: 16, of which 4 were waited for; matrix products, arithmetic and copies ran while one was open for 0% of the time, Pallas kernels for 0%

commit v1 on v0

v1 whole, which is shorter than its diff:
```python
import functools
import math

import jax
import jax.numpy as jnp
from jax import lax
from jax.experimental import pallas as pl
from jax.experimental.pallas import tpu as pltpu
from jax.sharding import PartitionSpec as P

kernel_norm = 21.0 / (16.0 * math.pi)
viscosity = 0.1
time_step = 0.02
rest_density = 1.0

MESH = pl.DeviceIdType.MESH
OWN = 2
BOXES = 5
BESIDE = (0, 1, 3, 4)
KDEPTH = 32
FEATURES = 16
UNROLL = 4

f32, bf16 = jnp.float32, jnp.bfloat16


def split_in(value, parts):
    pieces = []
    for _ in range(parts):
        piece = value.astype(bf16)
        pieces.append(piece)
        value = value - piece.astype(f32)
    return pieces


def dot_nn(a, b):
    return lax.dot_general(a, b, (((1,), (0,)), ((), ())), preferred_element_type=f32)


def dot_nt(a, b):
    return lax.dot_general(a, b, (((1,), (1,)), ((), ())), preferred_element_type=f32)


def kernel(
    gx, gy, tiles, size, rows,
    pos, vel, mass, stiff, counts, pairs_v, pairs_s, live_s,
    accel_out, density_out,
    pm, vs, side_a, side_b, mass_rows, feats, slope, row_density, row_force, picks,
    dens_part, dens_recv, dens_total, force_part, force_recv, send_sem, recv_sem,
):
    my_x, my_y = lax.axis_index("gx"), lax.axis_index("gy")
    where_to = {
        0: (lax.rem(my_x + gx - 1, gx), my_y),
        1: (my_x, lax.rem(my_y + gy - 1, gy)),
        3: (my_x, lax.rem(my_y + 1, gy)),
        4: (lax.rem(my_x + 1, gx), my_y),
    }
    all_tiles = BOXES * tiles

    barrier = pltpu.get_barrier_semaphore()
    for b in BESIDE:
        pl.semaphore_signal(barrier, inc=1, device_id=where_to[b], device_id_type=MESH)

    row_at = lax.broadcasted_iota(jnp.int32, (tiles, tiles), 0)
    column_at = lax.broadcasted_iota(jnp.int32, (tiles, tiles), 1)
    count = jnp.sum(
        jnp.where(row_at == column_at, counts[...].astype(f32), 0.0), axis=1, keepdims=True
    )
    lane = lax.broadcasted_iota(jnp.int32, (tiles, size), 1).astype(f32)
    for c in range(3):
        pm[OWN, c] = 0.5 * (pos[c] - 1.0)
        vs[OWN, c] = vel[c]
    pm[OWN, 3] = jnp.where(lane < count, mass[...], 0.0)
    vs[OWN, 3] = stiff[...]

    pl.semaphore_wait(barrier, len(BESIDE))

    def exchange(stage, source_of, target):
        copies = {}
        for b in BESIDE:
            copies[b] = pltpu.make_async_remote_copy(
                src_ref=source_of(b),
                dst_ref=target.at[4 - b],
                send_sem=send_sem.at[stage, b],
                recv_sem=recv_sem.at[stage, 4 - b],
                device_id=where_to[b],
                device_id_type=MESH,
            )
            copies[b].start()
        return copies

    def arrived(stage, b, target):
        pltpu.make_async_remote_copy(
            src_ref=target.at[b],
            dst_ref=target.at[b],
            send_sem=send_sem.at[stage, b],
            recv_sem=recv_sem.at[stage, b],
            device_id=where_to[b],
            device_id_type=MESH,
        ).wait_recv()

    sent = []
    sent.append(exchange(0, lambda b: pm.at[OWN], pm))
    sent.append(exchange(1, lambda b: vs.at[OWN], vs))

    def at_plane(ref, plane, b):
        return ref.at[pl.ds(plane * all_tiles + b * tiles, tiles)]

    def distance_planes(b):
        ones = jnp.ones((tiles, size), f32)
        norm = jnp.zeros((tiles, size), f32)
        planes_a, planes_b = [], []
        for c in range(3):
            h = pm[b, c]
            norm = norm + h * h
            h1, h2, h3 = (p.astype(f32) for p in split_in(h, 3))
            planes_a += [-2.0 * v for v in (h1, h1, h2, h2, h1, h3)]
            planes_b += [h1, h2, h1, h2, h3, h1]
        n_parts = [p.astype(f32) for p in split_in(norm, 3)]
        planes_a += n_parts + [ones] * 3
        planes_b += [ones] * 3 + n_parts
        if b in (0, OWN, 4):
            for k, value in enumerate(planes_a):
                at_plane(side_a, k, b)[...] = value
        if b in (1, OWN, 3):
            for k, value in enumerate(planes_b):
                at_plane(side_b, k, b)[...] = value
        for k, value in enumerate(split_in(pm[b, 3], 3)):
            at_plane(mass_rows, k, b)[...] = value.astype(f32)

    def zero_planes(ref, first, last):
        ref[pl.ds(first * all_tiles, (last - first) * all_tiles)] = jnp.zeros(
            ((last - first) * all_tiles, size), f32
        )

    distance_planes(OWN)
    zero_planes(side_a, 24, KDEPTH)
    zero_planes(side_b, 24, KDEPTH)
    zero_planes(mass_rows, 3, 8)
    for part in range(3):
        zero_planes(feats, part * FEATURES + 12, (part + 1) * FEATURES)
    row_density[pl.ds(rows, tiles)] = jnp.zeros((tiles, size), f32)
    for f in range(12):
        row_force[pl.ds(f * 2 * rows + rows, tiles)] = jnp.zeros((tiles, size), f32)

    first = pairs_v[0:1, :]
    second = pairs_v[1:2, :]
    row_index = lax.broadcasted_iota(jnp.int32, (1, rows), 1)
    live = row_index < live_s[0]

    def local_first(tile):
        return (OWN + 2 * (lax.div(tile, gy * tiles) - my_x)) * tiles + lax.rem(tile, tiles)

    def local_second(tile):
        return (OWN + lax.rem(lax.div(tile, tiles), gy) - my_y) * tiles + lax.rem(tile, tiles)

    to_first = jnp.where(live, local_first(first), -1)
    to_second = jnp.where(live & (first != second), local_second(second), -1)
    tile_at = lax.broadcasted_iota(jnp.int32, (all_tiles, rows), 0)
    picks[:, 0:rows] = jnp.where(tile_at == to_first, 1.0, 0.0).astype(bf16)
    picks[:, rows : 2 * rows] = jnp.where(tile_at == to_second, 1.0, 0.0).astype(bf16)

    def tile_rows(ref, tile, count):
        return ref[pl.ds(tile, count, stride=all_tiles), :].astype(bf16)

    def twice(value):
        return jnp.concatenate([value, value], axis=1)

    def density_row(r, t1, t2, cross):
        a = tile_rows(side_a, t1, KDEPTH)
        b = tile_rows(side_b, t2, KDEPTH)
        square = lax.dot_general(a, b, (((0,), (0,)), ((), ())), preferred_element_type=f32)
        square = jnp.maximum(square, 1e-13)
        fall = jnp.maximum(1.0 - square * lax.rsqrt(square), 0.0)
        fall2 = fall * fall
        weight_hi, weight_lo = split_in(fall2 * fall2 * (5.0 - 4.0 * fall), 2)
        slope_hi, slope_lo = split_in(fall2 * fall, 2)
        slope[r, :, 0:size] = slope_hi
        slope[r, :, size : 2 * size] = slope_lo
        beside = jnp.concatenate([weight_hi, weight_lo], axis=1)
        got = dot_nt(twice(tile_rows(mass_rows, t2, 8)), beside)
        row_density[pl.ds(r, 1)] = jnp.sum(got, axis=0, keepdims=True)
        if cross:
            below = jnp.concatenate([weight_hi, weight_lo], axis=0)
            got = dot_nn(twice(tile_rows(mass_rows, t1, 8)), below)
            row_density[pl.ds(rows + r, 1)] = jnp.sum(got, axis=0, keepdims=True)

    def force_row(r, t1, t2, cross):
        both = slope[r]

        def summed(got):
            return got[0:16] + got[16:32] + got[32:48]

        got = dot_nt(twice(tile_rows(feats, t2, 3 * FEATURES)), both)
        row_force[pl.ds(r, FEATURES, stride=2 * rows), :] = summed(got)
        if cross:
            below = jnp.concatenate([both[:, 0:size], both[:, size : 2 * size]], axis=0)
            got = dot_nn(twice(tile_rows(feats, t1, 3 * FEATURES)), below)
            row_force[pl.ds(rows + r, FEATURES, stride=2 * rows), :] = summed(got)

    def own_rows(work):
        def turn(step, carry):
            for u in range(UNROLL):
                r = step * UNROLL + u
                work(r, OWN * tiles + r, OWN * tiles + r, False)
            return carry

        lax.fori_loop(0, tiles // UNROLL, turn, 0)

    def cross_rows(work):
        def turn(step, carry):
            for u in range(UNROLL):
                r = tiles + step * UNROLL + u
                t1 = jnp.clip(local_first(pairs_s[0, r]), 0, all_tiles - 1)
                t2 = jnp.clip(local_second(pairs_s[1, r]), 0, all_tiles - 1)
                work(r, t1, t2, True)
            return carry

        lax.fori_loop(0, (rows - tiles) // UNROLL, turn, 0)

    own_rows(density_row)
    for b in BESIDE:
        arrived(0, b, pm)
        distance_planes(b)
    cross_rows(density_row)

    chosen = picks[...]
    total = jnp.zeros((all_tiles, size), f32)
    for part in split_in(row_density[...], 3):
        total = total + dot_nn(chosen, part)
    dens_part[...] = (kernel_norm * total).reshape(BOXES, tiles, size)
    sent.append(exchange(2, lambda b: dens_part.at[b], dens_recv))
    density = dens_part[OWN]
    for b in BESIDE:
        arrived(2, b, dens_recv)
        density = density + dens_recv[b]
    dens_total[OWN] = density
    density_out[...] = density
    sent.append(exchange(3, lambda b: dens_total.at[OWN], dens_total))

    def pressures(b):
        density = dens_total[b]
        scale = density + 1.0 - jnp.where(pm[b, 3] > 0.0, 1.0, 0.0)
        inverse = 1.0 / scale
        press = vs[b, 3] * (density - rest_density) * inverse * inverse
        return press, inverse

    def force_planes(b):
        press, inverse = pressures(b)
        m = pm[b, 3]
        mp, mq = m * press, m * inverse
        values = [m] + [m * pm[b, c] for c in range(3)]
        values += [mp] + [mp * pm[b, c] for c in range(3)]
        values += [mq] + [mq * vs[b, c] for c in range(3)]
        for k, value in enumerate(values):
            for part, piece in enumerate(split_in(value, 3)):
                at_plane(feats, part * FEATURES + k, b)[...] = piece.astype(f32)

    force_planes(OWN)
    own_rows(force_row)
    for b in BESIDE:
        arrived(1, b, vs)
        arrived(3, b, dens_total)
        force_planes(b)
    cross_rows(force_row)

    sums = []
    for f in range(12):
        total = jnp.zeros((all_tiles, size), f32)
        for part in split_in(row_force[pl.ds(f * 2 * rows, 2 * rows)], 3):
            total = total + dot_nn(chosen, part)
        sums.append(total)
    for b in range(BOXES):
        press, inverse = pressures(b)
        s = [v[b * tiles : (b + 1) * tiles] for v in sums]
        for c in range(3):
            h, v = pm[b, c], vs[b, c]
            push = press * (h * s[0] - s[1 + c]) + h * s[4] - s[5 + c]
            drag = inverse * (v * s[8] - s[9 + c])
            force_part[b, c] = (5.0 * kernel_norm) * (2.0 * push - (2.0 * viscosity) * drag)
    sent.append(exchange(4, lambda b: force_part.at[b], force_recv))
    accel = force_part[OWN]
    for b in BESIDE:
        arrived(4, b, force_recv)
        accel = accel + force_recv[b]
    accel_out[...] = accel * jnp.where(pm[OWN, 3] > 0.0, 1.0, 0.0)[None]

    for copies in sent:
        for b in BESIDE:
            copies[b].wait_send()


def body(gx, gy, positions, velocities, mass, stiffness, counts, pairs, pair_count):
    tiles = counts.shape[2]
    size = positions.shape[3] // tiles
    rows = pairs.shape[0]
    all_tiles = BOXES * tiles
    points = positions.reshape(3, tiles, size)
    speeds = velocities.reshape(3, tiles, size)
    turned = pairs.T
    vmem = pl.BlockSpec(memory_space=pltpu.VMEM)
    smem = pl.BlockSpec(memory_space=pltpu.SMEM)
    accel, density = pl.pallas_call(
        functools.partial(kernel, gx, gy, tiles, size, rows),
        out_shape=(
            jax.ShapeDtypeStruct((3, tiles, size), f32),
            jax.ShapeDtypeStruct((tiles, size), f32),
        ),
        in_specs=[vmem] * 6 + [smem] * 2,
        out_specs=(vmem, vmem),
        scratch_shapes=[
            pltpu.VMEM((BOXES, 4, tiles, size), f32),
            pltpu.VMEM((BOXES, 4, tiles, size), f32),
            pltpu.VMEM((KDEPTH * all_tiles, size), f32),
            pltpu.VMEM((KDEPTH * all_tiles, size), f32),
            pltpu.VMEM((8 * all_tiles, size), f32),
            pltpu.VMEM((3 * FEATURES * all_tiles, size), f32),
            pltpu.VMEM((rows, size, 2 * size), bf16),
            pltpu.VMEM((2 * rows, size), f32),
            pltpu.VMEM((FEATURES * 2 * rows, size), f32),
            pltpu.VMEM((all_tiles, 2 * rows), bf16),
            pltpu.VMEM((BOXES, tiles, size), f32),
            pltpu.VMEM((BOXES, tiles, size), f32),
            pltpu.VMEM((BOXES, tiles, size), f32),
            pltpu.VMEM((BOXES, 3, tiles, size), f32),
            pltpu.VMEM((BOXES, 3, tiles, size), f32),
            pltpu.SemaphoreType.DMA((5, BOXES)),
            pltpu.SemaphoreType.DMA((5, BOXES)),
        ],
        compiler_params=pltpu.CompilerParams(collective_id=0, has_side_effects=True),
        name="sph_step",
    )(
        points,
        speeds,
        mass.reshape(tiles, size),
        stiffness.reshape(tiles, size),
        counts.reshape(1, tiles),
        turned,
        turned,
        pair_count,
    )
    new_speeds = speeds + time_step * accel
    new_points = points + time_step * new_speeds
    return (
        new_points.reshape(positions.shape),
        new_speeds.reshape(velocities.shape),
        density.reshape(mass.shape),
    )


def solution(mesh):
    placed = (
        P(None, "gx", "gy", None),
        P(None, "gx", "gy", None),
        P("gx", "gy", None),
        P("gx", "gy", None),
        P("gx", "gy", None),
        P(("gx", "gy"), None),
        P(("gx", "gy")),
    )
    return jax.shard_map(
        functools.partial(body, mesh.shape["gx"], mesh.shape["gy"]),
        mesh=mesh,
        in_specs=placed,
        out_specs=(P(None, "gx", "gy", None), P(None, "gx", "gy", None), P("gx", "gy", None)),
        check_vma=False,
    )
```

time: 260 us -> 65.3 us (0.25)
  the two profiles are of different devices: /device:TPU:33 before, /device:TPU:2 now
where the time goes in v1:
time: 65.3 us; the launch traced here: 65.1 us
  Pallas kernels  61.7 us (94%)
  other arithmetic  1.45 us (2%)
  between operations  1.33 us (2%)
    pallas_call x1, Pallas kernels, body(): pl.pallas_call(functools.partial(kernel, gx, gy, tiles, size, rows), out_...  61.7 us
    add x1, other arithmetic, body(): new_points = points + time_step * new_speeds  1.45 us

profile of v1, /device:TPU:2, one launch (start us, length us, event | category | flops | bytes accessed | tf_op | source)
XLA Modules:
  0.0 65.1 jit_solution(9206362039876009599)
XLA Ops:
  1.3 0.0 copy-start
  1.3 0.0 copy-start.1
  1.3 61.7 %sph_step.1 = (f32[3,32,128]{2,1,0:T(8,128)}, f32[32,128]{1,0:T(8,128)}) custom-call(f32[3,32,128]{2,1,0:T(8,128)} %bitcast.9, f32[3,32,128]{2,1,0:T(8,128)} %bitcast.11, f32[32,128]{1,0:T(8,128)} %bitcast.16, f32[32,128]{1,0:T(8,128)} %bitcast.17, s32[1,32]{1,0:T(1,128)} %bitcast.20, s32[2,128]{1,0:T(2,128)} %bitcast.18, s32[2,128]{1,0:T(2,128)} %bitcast.19, ...), custom_call_target="tpu_custom_call" | custom-call | tf_op jit(solution)/shard_map/sph_step/pallas_call | solution.py:303
  63.0 0.0 copy-done
  63.0 0.0 copy-done.1
  63.0 0.0 copy-start.2
  63.0 1.4 %multiply_add_fusion = (f32[3,32,128]{2,1,0:T(8,128)}, f32[3,32,128]{2,1,0:T(8,128)}) fusion(f32[3,32,128]{2,1,0:T(8,128)S(1)} %bitcast.10, f32[3,32,128]{2,1,0:T(8,128)S(1)} %bitcast.12, f32[3,32,128]{2,1,0:T(8,128)} %get-tuple-element.5), kind=kLoop, calls=%fused_computation | loop fusion | flops 49152 | bytes 245760 | tf_op jit(solution)/shard_map/add | solution.py:343
  64.5 0.0 copy-done.2
  64.5 0.6 copy.16
Async XLA Ops:
  1.3 61.7 %copy-start = (f32[3,1,1,4096]{3,2,1,0:T(1,128)S(1)}, f32[3,1,1,4096]{3,2,1,0:T(1,128)}, u32[]{:S(2)}) copy-start(f32[3,1,1,4096]{3,2,1,0:T(1,128)} %param.7) | copy-start | bytes 147460
  1.3 61.7 %copy-start.1 = (f32[3,1,1,4096]{3,2,1,0:T(1,128)S(1)}, f32[3,1,1,4096]{3,2,1,0:T(1,128)}, u32[]{:S(2)}) copy-start(f32[3,1,1,4096]{3,2,1,0:T(1,128)} %param.8) | copy-start | bytes 147460
  63.0 1.5 %copy-start.2 = (f32[32,128]{1,0:T(8,128)S(1)}, f32[32,128]{1,0:T(8,128)}, u32[]{:S(2)}) copy-start(f32[32,128]{1,0:T(8,128)} %get-tuple-element.6) | copy-start | bytes 49156

commit v2 on v1

--- a/solution.py
+++ b/solution.py
@@ -17,9 +17,10 @@
 OWN = 2
 BOXES = 5
 BESIDE = (0, 1, 3, 4)
-KDEPTH = 32
+KDEPTH = 24
 FEATURES = 16
 UNROLL = 4
+FORCE_UNROLL = 8
 
 f32, bf16 = jnp.float32, jnp.bfloat16
 
@@ -43,9 +44,10 @@
 
 def kernel(
     gx, gy, tiles, size, rows,
-    pos, vel, mass, stiff, counts, pairs_v, pairs_s, live_s,
+    pos, vel, mass, stiff, counts, pairs_v, live_s,
     accel_out, density_out,
-    pm, vs, side_a, side_b, mass_rows, feats, slope, row_density, row_force, picks,
+    pm, vs, side_a, side_b, mass_rows, feats, squares, weights, falls, slope,
+    row_density, row_force, picks, table_v, table_s, table_sem,
     dens_part, dens_recv, dens_total, force_part, force_recv, send_sem, recv_sem,
 ):
     my_x, my_y = lax.axis_index("gx"), lax.axis_index("gy")
@@ -56,6 +58,7 @@
         4: (lax.rem(my_x + 1, gx), my_y),
     }
     all_tiles = BOXES * tiles
+    plane_step, force_step = all_tiles + 1, 2 * rows + 1
 
     barrier = pltpu.get_barrier_semaphore()
     for b in BESIDE:
@@ -104,7 +107,7 @@
     sent.append(exchange(1, lambda b: vs.at[OWN], vs))
 
     def at_plane(ref, plane, b):
-        return ref.at[pl.ds(plane * all_tiles + b * tiles, tiles)]
+        return ref.at[pl.ds(plane * plane_step + b * tiles, tiles)]
 
     def distance_planes(b):
         ones = jnp.ones((tiles, size), f32)
@@ -125,111 +128,132 @@
         if b in (1, OWN, 3):
             for k, value in enumerate(planes_b):
                 at_plane(side_b, k, b)[...] = value
-        for k, value in enumerate(split_in(pm[b, 3], 3)):
+        for k, value in enumerate(split_in(pm[b, 3], 2)):
             at_plane(mass_rows, k, b)[...] = value.astype(f32)
 
-    def zero_planes(ref, first, last):
-        ref[pl.ds(first * all_tiles, (last - first) * all_tiles)] = jnp.zeros(
-            ((last - first) * all_tiles, size), f32
-        )
-
     distance_planes(OWN)
-    zero_planes(side_a, 24, KDEPTH)
-    zero_planes(side_b, 24, KDEPTH)
-    zero_planes(mass_rows, 3, 8)
-    for part in range(3):
-        zero_planes(feats, part * FEATURES + 12, (part + 1) * FEATURES)
     row_density[pl.ds(rows, tiles)] = jnp.zeros((tiles, size), f32)
     for f in range(12):
-        row_force[pl.ds(f * 2 * rows + rows, tiles)] = jnp.zeros((tiles, size), f32)
+        row_force[pl.ds(f * force_step + rows, tiles)] = jnp.zeros((tiles, size), f32)
 
     first = pairs_v[0:1, :]
     second = pairs_v[1:2, :]
     row_index = lax.broadcasted_iota(jnp.int32, (1, rows), 1)
     live = row_index < live_s[0]
 
-    def local_first(tile):
-        return (OWN + 2 * (lax.div(tile, gy * tiles) - my_x)) * tiles + lax.rem(tile, tiles)
-
-    def local_second(tile):
-        return (OWN + lax.rem(lax.div(tile, tiles), gy) - my_y) * tiles + lax.rem(tile, tiles)
-
-    to_first = jnp.where(live, local_first(first), -1)
-    to_second = jnp.where(live & (first != second), local_second(second), -1)
+    first_tile = (OWN + 2 * (lax.div(first, gy * tiles) - my_x)) * tiles + lax.rem(first, tiles)
+    second_tile = (OWN + lax.rem(lax.div(second, tiles), gy) - my_y) * tiles + lax.rem(second, tiles)
+    to_first = jnp.where(live, first_tile, -1)
+    to_second = jnp.where(live & (first != second), second_tile, -1)
     tile_at = lax.broadcasted_iota(jnp.int32, (all_tiles, rows), 0)
     picks[:, 0:rows] = jnp.where(tile_at == to_first, 1.0, 0.0).astype(bf16)
     picks[:, rows : 2 * rows] = jnp.where(tile_at == to_second, 1.0, 0.0).astype(bf16)
+    table_v[0:1] = jnp.clip(first_tile, 0, all_tiles - 1)
+    table_v[1:2] = jnp.clip(second_tile, 0, all_tiles - 1)
+    table_copy = pltpu.make_async_copy(table_v, table_s, table_sem)
+    table_copy.start()
+
+    def own_tiles(r):
+        return OWN * tiles + r, OWN * tiles + r
+
+    def listed_tiles(r):
+        return table_s[0, r], table_s[1, r]
 
     def tile_rows(ref, tile, count):
-        return ref[pl.ds(tile, count, stride=all_tiles), :].astype(bf16)
+        return ref[pl.ds(tile, count, stride=plane_step), :].astype(bf16)
 
     def twice(value):
         return jnp.concatenate([value, value], axis=1)
 
-    def density_row(r, t1, t2, cross):
+    def side_by_side(value):
+        return jnp.concatenate([value[0:size], value[size : 2 * size]], axis=1)
+
+    def distances(u, t1, t2):
         a = tile_rows(side_a, t1, KDEPTH)
         b = tile_rows(side_b, t2, KDEPTH)
-        square = lax.dot_general(a, b, (((0,), (0,)), ((), ())), preferred_element_type=f32)
-        square = jnp.maximum(square, 1e-13)
+        squares[u] = lax.dot_general(a, b, (((0,), (0,)), ((), ())), preferred_element_type=f32)
+
+    def weigh(r, u):
+        square = jnp.maximum(squares[u], 1e-13)
         fall = jnp.maximum(1.0 - square * lax.rsqrt(square), 0.0)
         fall2 = fall * fall
-        weight_hi, weight_lo = split_in(fall2 * fall2 * (5.0 - 4.0 * fall), 2)
-        slope_hi, slope_lo = split_in(fall2 * fall, 2)
-        slope[r, :, 0:size] = slope_hi
-        slope[r, :, size : 2 * size] = slope_lo
-        beside = jnp.concatenate([weight_hi, weight_lo], axis=1)
-        got = dot_nt(twice(tile_rows(mass_rows, t2, 8)), beside)
-        row_density[pl.ds(r, 1)] = jnp.sum(got, axis=0, keepdims=True)
+        falls[r] = fall
+        weight_hi, weight_lo = split_in(fall2 * fall2 * (1.25 - fall), 2)
+        weights[u, 0:size] = weight_hi
+        weights[u, size : 2 * size] = weight_lo
+
+    def add_up(r, u, t1, t2, cross):
+        both = weights[u]
+        got = dot_nt(twice(tile_rows(mass_rows, t2, 8)), side_by_side(both))
+        row_density[pl.ds(r, 1)] = got[0:1] + got[1:2]
         if cross:
-            below = jnp.concatenate([weight_hi, weight_lo], axis=0)
-            got = dot_nn(twice(tile_rows(mass_rows, t1, 8)), below)
-            row_density[pl.ds(rows + r, 1)] = jnp.sum(got, axis=0, keepdims=True)
+            got = dot_nn(twice(tile_rows(mass_rows, t1, 8)), both)
+            row_density[pl.ds(rows + r, 1)] = got[0:1] + got[1:2]
+
+    def density_rows(start, end, tiles_of, cross):
+        for u in range(UNROLL):
+            distances(u, *tiles_of(start + u))
+
+        def turn(step, carry):
+            for u in range(UNROLL):
+                r = start + step * UNROLL + u
+                before = jnp.maximum(r - UNROLL, start)
+                spare = jnp.where(step == 0, 2 * rows + u, before)
+                add_up(spare, u, *tiles_of(before), cross)
+                weigh(r, u)
+                distances(u, *tiles_of(jnp.minimum(r + UNROLL, end - 1)))
+            return carry
+
+        lax.fori_loop(0, (end - start) // UNROLL, turn, 0)
+        for u in range(UNROLL):
+            r = end - UNROLL + u
+            add_up(r, u, *tiles_of(r), cross)
+
+    def slopes(start, end):
+        def turn(step, carry):
+            for u in range(4):
+                r = start + step * 4 + u
+                fall = falls[r]
+                slope_hi, slope_lo = split_in(fall * fall * fall, 2)
+                slope[r, 0:size] = slope_hi
+                slope[r, size : 2 * size] = slope_lo
+            return carry
+
+        lax.fori_loop(0, (end - start) // 4, turn, 0)
 
     def force_row(r, t1, t2, cross):
         both = slope[r]
-
-        def summed(got):
-            return got[0:16] + got[16:32] + got[32:48]
-
-        got = dot_nt(twice(tile_rows(feats, t2, 3 * FEATURES)), both)
-        row_force[pl.ds(r, FEATURES, stride=2 * rows), :] = summed(got)
+        got = dot_nt(twice(tile_rows(feats, t2, 2 * FEATURES)), side_by_side(both))
+        row_force[pl.ds(r, FEATURES, stride=force_step), :] = got[0:FEATURES] + got[FEATURES:]
         if cross:
-            below = jnp.concatenate([both[:, 0:size], both[:, size : 2 * size]], axis=0)
-            got = dot_nn(twice(tile_rows(feats, t1, 3 * FEATURES)), below)
-            row_force[pl.ds(rows + r, FEATURES, stride=2 * rows), :] = summed(got)
-
-    def own_rows(work):
+            got = dot_nn(twice(tile_rows(feats, t1, 2 * FEATURES)), both)
+            row_force[pl.ds(rows + r, FEATURES, stride=force_step), :] = (
+                got[0:FEATURES] + got[FEATURES:]
+            )
+
+    def force_rows(start, end, tiles_of, cross):
         def turn(step, carry):
-            for u in range(UNROLL):
-                r = step * UNROLL + u
-                work(r, OWN * tiles + r, OWN * tiles + r, False)
+            for u in range(FORCE_UNROLL):
+                r = start + step * FORCE_UNROLL + u
+                force_row(r, *tiles_of(r), cross)
             return carry
 
-        lax.fori_loop(0, tiles // UNROLL, turn, 0)
-
-    def cross_rows(work):
-        def turn(step, carry):
-            for u in range(UNROLL):
-                r = tiles + step * UNROLL + u
-                t1 = jnp.clip(local_first(pairs_s[0, r]), 0, all_tiles - 1)
-                t2 = jnp.clip(local_second(pairs_s[1, r]), 0, all_tiles - 1)
-                work(r, t1, t2, True)
-            return carry
-
-        lax.fori_loop(0, (rows - tiles) // UNROLL, turn, 0)
-
-    own_rows(density_row)
+        lax.fori_loop(0, (end - start) // FORCE_UNROLL, turn, 0)
+
+    density_rows(0, tiles, own_tiles, False)
+    table_copy.wait()
     for b in BESIDE:
         arrived(0, b, pm)
         distance_planes(b)
-    cross_rows(density_row)
+    density_rows(tiles, rows, listed_tiles, True)
 
     chosen = picks[...]
     total = jnp.zeros((all_tiles, size), f32)
-    for part in split_in(row_density[...], 3):
+    for part in split_in(row_density[0 : 2 * rows], 3):
         total = total + dot_nn(chosen, part)
-    dens_part[...] = (kernel_norm * total).reshape(BOXES, tiles, size)
+    dens_part[...] = ((4.0 * kernel_norm) * total).reshape(BOXES, tiles, size)
     sent.append(exchange(2, lambda b: dens_part.at[b], dens_recv))
+    slopes(0, rows // 2)
     density = dens_part[OWN]
     for b in BESIDE:
         arrived(2, b, dens_recv)
@@ -253,23 +277,27 @@
         values += [mp] + [mp * pm[b, c] for c in range(3)]
         values += [mq] + [mq * vs[b, c] for c in range(3)]
         for k, value in enumerate(values):
-            for part, piece in enumerate(split_in(value, 3)):
+            for part, piece in enumerate(split_in(value, 2)):
                 at_plane(feats, part * FEATURES + k, b)[...] = piece.astype(f32)
 
+    slopes(rows // 2, rows)
     force_planes(OWN)
-    own_rows(force_row)
+    force_rows(0, tiles, own_tiles, False)
     for b in BESIDE:
         arrived(1, b, vs)
         arrived(3, b, dens_total)
         force_planes(b)
-    cross_rows(force_row)
+    force_rows(tiles, rows, listed_tiles, True)
 
     sums = []
-    for f in range(12):
-        total = jnp.zeros((all_tiles, size), f32)
-        for part in split_in(row_force[pl.ds(f * 2 * rows, 2 * rows)], 3):
-            total = total + dot_nn(chosen, part)
-        sums.append(total)
+    for f in range(0, 12, 2):
+        pair = [split_in(row_force[pl.ds((f + k) * force_step, 2 * rows)], 2) for k in range(2)]
+        total = jnp.zeros((all_tiles, 2 * size), f32)
+        for part in range(2):
+            total = total + dot_nn(
+                chosen, jnp.concatenate([pair[0][part], pair[1][part]], axis=1)
+            )
+        sums += [total[:, 0:size], total[:, size:]]
     for b in range(BOXES):
         press, inverse = pressures(b)
         s = [v[b * tiles : (b + 1) * tiles] for v in sums]
@@ -306,19 +334,25 @@
             jax.ShapeDtypeStruct((3, tiles, size), f32),
             jax.ShapeDtypeStruct((tiles, size), f32),
         ),
-        in_specs=[vmem] * 6 + [smem] * 2,
+        in_specs=[vmem] * 6 + [smem],
         out_specs=(vmem, vmem),
         scratch_shapes=[
             pltpu.VMEM((BOXES, 4, tiles, size), f32),
             pltpu.VMEM((BOXES, 4, tiles, size), f32),
-            pltpu.VMEM((KDEPTH * all_tiles, size), f32),
-            pltpu.VMEM((KDEPTH * all_tiles, size), f32),
-            pltpu.VMEM((8 * all_tiles, size), f32),
-            pltpu.VMEM((3 * FEATURES * all_tiles, size), f32),
-            pltpu.VMEM((rows, size, 2 * size), bf16),
-            pltpu.VMEM((2 * rows, size), f32),
-            pltpu.VMEM((FEATURES * 2 * rows, size), f32),
+            pltpu.VMEM((KDEPTH * (all_tiles + 1), size), f32),
+            pltpu.VMEM((KDEPTH * (all_tiles + 1), size), f32),
+            pltpu.VMEM((8 * (all_tiles + 1), size), f32),
+            pltpu.VMEM((2 * FEATURES * (all_tiles + 1), size), f32),
+            pltpu.VMEM((UNROLL, size, size), f32),
+            pltpu.VMEM((UNROLL, 2 * size, size), bf16),
+            pltpu.VMEM((rows, size, size), f32),
+            pltpu.VMEM((rows, 2 * size, size), bf16),
+            pltpu.VMEM((3 * rows + 8, size), f32),
+            pltpu.VMEM((FEATURES * (2 * rows + 1), size), f32),
             pltpu.VMEM((all_tiles, 2 * rows), bf16),
+            pltpu.VMEM((2, rows), jnp.int32),
+            pltpu.SMEM((2, rows), jnp.int32),
+            pltpu.SemaphoreType.DMA,
             pltpu.VMEM((BOXES, tiles, size), f32),
             pltpu.VMEM((BOXES, tiles, size), f32),
             pltpu.VMEM((BOXES, tiles, size), f32),
@@ -336,7 +370,6 @@
         stiffness.reshape(tiles, size),
         counts.reshape(1, tiles),
         turned,
-        turned,
         pair_count,
     )
     new_speeds = speeds + time_step * accel

time: 65.3 us -> 46.6 us (0.71)
  Pallas kernels: 61.7 us -> 42.9 us
    pallas_call x1, Pallas kernels: 61.7 us -> 42.9 us  [body(): pl.pallas_call(functools.partial(kernel, gx, gy, tiles, size, rows), out_...]
where the time goes in v2:
time: 46.6 us; the launch traced here: 46.3 us
  Pallas kernels  42.9 us (92%)
  other arithmetic  1.45 us (3%)
  between operations  1.33 us (3%)
  local copies, waits for them, and re-layouts  0.62 us (1%)
    pallas_call x1, Pallas kernels, body(): pl.pallas_call(functools.partial(kernel, gx, gy, tiles, size, rows), out_...  42.9 us
    add x1, other arithmetic, body(): new_points = points + time_step * new_speeds  1.45 us

profile of v2, /device:TPU:2, one launch (start us, length us, event | category | flops | bytes accessed | tf_op | source)
XLA Modules:
  0.0 46.3 jit_solution(7314348740232553657)
XLA Ops:
  1.3 0.0 copy-start
  1.3 0.0 copy-start.1
  1.3 42.9 %sph_step.1 = (f32[3,32,128]{2,1,0:T(8,128)}, f32[32,128]{1,0:T(8,128)}) custom-call(f32[3,32,128]{2,1,0:T(8,128)} %bitcast.9, f32[3,32,128]{2,1,0:T(8,128)} %bitcast.11, f32[32,128]{1,0:T(8,128)} %bitcast.16, f32[32,128]{1,0:T(8,128)} %bitcast.17, s32[1,32]{1,0:T(1,128)} %bitcast.19, s32[2,128]{1,0:T(2,128)} %bitcast.18, s32[1]{0:T(128)S(6)} %copy.15.live_s), custom_call_target="tpu_custom_call" | custom-call | tf_op jit(solution)/shard_map/sph_step/pallas_call | solution.py:331
  44.2 0.0 copy-done
  44.2 0.0 copy-done.1
  44.2 0.0 copy-start.2
  44.3 1.4 %multiply_add_fusion = (f32[3,32,128]{2,1,0:T(8,128)}, f32[3,32,128]{2,1,0:T(8,128)}) fusion(f32[3,32,128]{2,1,0:T(8,128)S(1)} %bitcast.10, f32[3,32,128]{2,1,0:T(8,128)S(1)} %bitcast.12, f32[3,32,128]{2,1,0:T(8,128)} %get-tuple-element.5), kind=kLoop, calls=%fused_computation | loop fusion | flops 49152 | bytes 245760 | tf_op jit(solution)/shard_map/add | solution.py:376
  45.7 0.0 copy-done.2
  45.7 0.6 %copy.16 = f32[1,1,4096]{2,1,0:T(1,128)} copy(f32[1,1,4096]{2,1,0:T(1,128)S(1)} %bitcast.15) | data formatting | bytes 32768
Async XLA Ops:
  1.3 42.9 %copy-start = (f32[3,1,1,4096]{3,2,1,0:T(1,128)S(1)}, f32[3,1,1,4096]{3,2,1,0:T(1,128)}, u32[]{:S(2)}) copy-start(f32[3,1,1,4096]{3,2,1,0:T(1,128)} %param.7) | copy-start | bytes 147460
  1.3 42.9 %copy-start.1 = (f32[3,1,1,4096]{3,2,1,0:T(1,128)S(1)}, f32[3,1,1,4096]{3,2,1,0:T(1,128)}, u32[]{:S(2)}) copy-start(f32[3,1,1,4096]{3,2,1,0:T(1,128)} %param.8) | copy-start | bytes 147460
  44.2 1.5 %copy-start.2 = (f32[32,128]{1,0:T(8,128)S(1)}, f32[32,128]{1,0:T(8,128)}, u32[]{:S(2)}) copy-start(f32[32,128]{1,0:T(8,128)} %get-tuple-element.6) | copy-start | bytes 49156
